TPU v7x, 32 devices: a whole 2x2x4 slice. The times are simulated.
32 devices in a mesh: vp: 8 (over z, x), op: 4 (over y, core).
Axes of the slice: x: 2, y: 2, z: 4, core: 2. Of those that a mesh axis runs over, the one named last changes fastest.
Arguments:
- amplitudes: bfloat16 [128, 8192], P('op', 'vp'), may hold values from -6 to 6
- driving_term: bfloat16 [128, 8192], P('op', 'vp'), may hold values from -6 to 6
- blocks: bfloat16 [8, 8, 1024, 1024], P('vp', None, 'op'), may hold values from -0.09375 to 0.09375
- block_tile: int32 [8, 8], P('vp'), may hold values from -1 to 7, as said below
- occupied_energy: float32 [128], P('op'), may hold values from 0.5 to 1.5
- virtual_energy: float32 [8192], P('vp'), may hold values from 1 to 3
Outputs:
- amplitudes_next: bfloat16 [128, 8192], P('op', 'vp')
Inputs may be any that keep to these rules, and one draw needn't show every extreme that they name: `block_tile`: row a lists slot 0 = a, then distinct tiles within 4 of a in no particular order, then -1 in the unused slots; at least one row uses all 8 slots.
All inputs are finite; a program needn't handle non-finite values.
Results may differ from a plain program's by a relative error of at most 0.0035.
Values may be sent and summed in bfloat16 or wider, within the bound.
A program may use at most 64 MiB of HBM per device.

v0:
```python
import jax
import jax.numpy as jnp
from jax import lax
from jax.sharding import PartitionSpec as P

ITERS = 2


def gather_listed(slices, listed):
    shards = lax.all_gather(slices[None], "vp", axis=0, tiled=True)
    owners = jnp.arange(shards.shape[0], dtype=jnp.int32)
    matches = (listed[:, None] == owners[None, :]).astype(jnp.bfloat16)
    picked = jnp.einsum("kj,jmc->kmc", matches, shards, preferred_element_type=jnp.float32)
    return picked.astype(jnp.bfloat16)


def per_device(amplitudes, driving_term, blocks, block_tile, occupied_energy, virtual_energy):
    listed = block_tile[0]
    integral_panel = blocks[0]
    inverse = 1.0 / (occupied_energy[:, None] + virtual_energy[None, :])
    driving = driving_term.astype(jnp.float32)
    current = amplitudes
    for iteration in range(ITERS):
        slices = lax.all_to_all(current, "op", split_axis=1, concat_axis=0, tiled=True)
        chosen = gather_listed(slices, listed)
        partial_value = jnp.einsum(
            "kmc,kcn->mn", chosen, integral_panel, preferred_element_type=jnp.float32
        )
        ladder = lax.psum_scatter(partial_value, "op", scatter_dimension=0, tiled=True)
        current = ((driving + ladder) * inverse).astype(jnp.bfloat16)
    return current


def solution(mesh):
    in_specs = (
        P("op", "vp"),
        P("op", "vp"),
        P("vp", None, "op", None),
        P("vp", None),
        P("op"),
        P("vp"),
    )
    out_specs = P("op", "vp")
    return jax.shard_map(
        per_device, mesh=mesh, in_specs=in_specs, out_specs=out_specs, check_vma=False
    )
```

profile of v0, /device:TPU:0, one launch (start us, length us, event | category | flops | bytes accessed | tf_op | source)
XLA Modules:
  0.0 147.7 jit_solution(5259783329638686071)
XLA Ops:
  6.5 0.0 copy-start.1
  6.5 0.0 copy-start.3
  6.5 0.0 copy-start
  6.5 0.0 reduce-scatter.3.cloned.1.call-start
  6.5 0.9 copy.33
  7.4 8.2 %all_to_all.32 = bf16[32,4,256]{2,0,1:T(8,128)(2,1)S(1)} all-to-all(bf16[32,4,256]{2,0,1:T(8,128)(2,1)S(1)} %bitcast.35), channel_id=1, replica_groups=mesh['vp'=8,'op'=4] {'op'}, dimensions={1} | all-to-all | bytes 131072 | tf_op jit(solution)/shard_map/all_to_all | solution.py:24
  15.6 0.0 copy-start.2
  15.6 31.9 %all_gather.6 = bf16[8,128,256]{2,1,0:T(8,128)(2,1)S(1)} all-gather(bf16[1,128,256]{2,1,0:T(8,128)(2,1)S(1)} %bitcast.32), channel_id=1, replica_groups=mesh['vp'=8,'op'=4] {'vp'}, dimensions={0}, use_global_device_ids=true | all-gather | bytes 589824 | tf_op jit(solution)/shard_map/all_gather | solution.py:10
  47.5 1.1 convolution_convert_fusion.1
  48.6 3.7 %fusion.4 = f32[128,1024]{1,0:T(8,128)} fusion(bf16[1,8,256,1024]{3,2,1,0:T(8,128)(2,1)} %param.8, bf16[8,128,256]{2,0,1:T(8,128)(2,1)S(1)} %convolution_convert_fusion.1), kind=kOutput, calls=%fused_computation.6 | convolution fusion | flops 536870912 | bytes 5242880 | tf_op jit(solution)/shard_map/kmc,kcn->mn/dot_general | solution.py:26
  52.3 0.0 reduce-scatter.3.cloned.1.call-update
  52.3 0.0 reduce-scatter.5.cloned.1.call-start
  52.4 21.8 %reduce-scatter.3.cloned.1.call-done = f32[32,1024]{1,0:T(8,128)} async-done(((f32[128,1024]{1,0:T(8,128)}), f32[32,1024]{1,0:T(8,128)}) %reduce-scatter.3.cloned.1.call-update) | async-done | bytes 131088 | tf_op jit(solution)/shard_map/reduce_scatter | solution.py:29
  74.2 0.0 copy-done.1
  74.2 0.0 copy-done.3
  74.2 0.0 copy-done
  74.2 1.0 fusion.15
  75.2 6.5 %all_to_all.33 = bf16[32,4,256]{2,0,1:T(8,128)(2,1)S(1)} all-to-all(bf16[32,4,256]{2,0,1:T(8,128)(2,1)S(1)} %bitcast.34), channel_id=1, replica_groups=mesh['vp'=8,'op'=4] {'op'}, dimensions={1} | all-to-all | bytes 131072 | tf_op jit(solution)/shard_map/all_to_all | solution.py:24
  81.7 31.5 %all_gather.7 = bf16[8,128,256]{2,1,0:T(8,128)(2,1)S(1)} all-gather(bf16[1,128,256]{2,1,0:T(8,128)(2,1)S(1)} %bitcast.33), channel_id=1, replica_groups=mesh['vp'=8,'op'=4] {'vp'}, dimensions={0}, use_global_device_ids=true | all-gather | bytes 589824 | tf_op jit(solution)/shard_map/all_gather | solution.py:10
  113.2 0.0 copy-done.2
  113.2 0.4 convolution_convert_fusion
  113.6 3.7 %fusion.7 = f32[128,1024]{1,0:T(8,128)} fusion(bf16[1,8,256,1024]{3,2,1,0:T(8,128)(2,1)} %param.8, bf16[8,128,256]{2,0,1:T(8,128)(2,1)S(1)} %convolution_convert_fusion), kind=kOutput, calls=%fused_computation.7 | convolution fusion | flops 536870912 | bytes 5242880 | tf_op jit(solution)/shard_map/kmc,kcn->mn/dot_general | solution.py:26
  117.4 0.0 reduce-scatter.5.cloned.1.call-update
  117.4 21.9 %reduce-scatter.5.cloned.1.call-done = f32[32,1024]{1,0:T(8,128)} async-done(((f32[128,1024]{1,0:T(8,128)}), f32[32,1024]{1,0:T(8,128)}) %reduce-scatter.5.cloned.1.call-update) | async-done | bytes 131088 | tf_op jit(solution)/shard_map/reduce_scatter | solution.py:29
  139.2 1.6 %fusion.17 = bf16[32,1024]{1,0:T(8,128)(2,1)} fusion(f32[32,1024]{1,0:T(8,128)} %reduce-scatter.5.cloned.1.call-done, bf16[32,1024]{1,0:T(8,128)(2,1)S(1)} %copy-done, f32[1024]{0:T(1024)S(1)} %copy-done.1, f32[32]{0:T(128)S(1)} %copy-done.3), kind=kLoop, calls=%fused_computation.17 | loop fusion | flops 196608 | bytes 266368 | tf_op jit(solution)/shard_map/convert_element_type | solution.py:30
  (1 shorter events, 0.0 us)
Async XLA Ops:
  6.5 67.7 %copy-start.1 = (f32[1024]{0:T(1024)S(1)}, f32[1024]{0:T(1024)}, u32[]{:S(2)}) copy-start(f32[1024]{0:T(1024)} %param.11) | copy-start | bytes 12292
  6.5 67.7 %copy-start.3 = (f32[32]{0:T(128)S(1)}, f32[32]{0:T(128)}, u32[]{:S(2)}) copy-start(f32[32]{0:T(128)} %param.10) | copy-start | bytes 388
  6.5 67.7 %copy-start = (bf16[32,1024]{1,0:T(8,128)(2,1)S(1)}, bf16[32,1024]{1,0:T(8,128)(2,1)}, u32[]{:S(2)}) copy-start(bf16[32,1024]{1,0:T(8,128)(2,1)} %param.7) | copy-start | bytes 196612
  6.5 67.7 %reduce-scatter.3.cloned.1.call-start = ((), (), s32[]{:S(2)}) async-start(), calls=%async_computation.4 | async-start | bytes 655360 | tf_op jit(solution)/shard_map/reduce_scatter | solution.py:29
  15.6 97.6 %copy-start.2 = (s32[1,8]{1,0:T(1,128)S(1)}, s32[1,8]{1,0:T(1,128)}, u32[]{:S(2)}) copy-start(s32[1,8]{1,0:T(1,128)} %param.9) | copy-start | bytes 100
  52.3 86.9 %reduce-scatter.5.cloned.1.call-start = ((), (), s32[]{:S(2)}) async-start(), calls=%async_computation.5 | async-start | bytes 655360 | tf_op jit(solution)/shard_map/reduce_scatter | solution.py:29
Sparse Core Ops, SparseCore 0:
  52.4 21.7 reduce-scatter.2
  117.5 21.6 reduce-scatter.4
where the time goes:
time: 148 us
  blocking collectives  78 us (53%)
  waiting for transfers between devices  43.7 us (30%)
  between operations  13.4 us (9%)
  matrix products  8.92 us (6%)
  other arithmetic  2.62 us (2%)
    all_gather x2, blocking collectives, gather_listed(): shards = lax.all_gather(slices[None], 'vp', axis=0, tiled=True)  63.4 us
    reduce_scatter x2, waiting for transfers between devices, per_device(): lax.psum_scatter(partial_value, 'op', scatter_dimension=0, tiled=True)  43.7 us
    all_to_all x2, blocking collectives, per_device(): lax.all_to_all(current, 'op', split_axis=1, concat_axis=0, tiled=True)  14.7 us
    dot_general x2, matrix products, per_device(): jnp.einsum('kmc,kcn->mn', chosen, integral_panel, preferred_element_type=...  7.43 us
  transfers between devices with their start and end apart: 2, of which 2 were waited for; matrix products, arithmetic and copies ran while one was open for 0% of the time, Pallas kernels for 0%

commit v1 on v0

v1 whole, which is shorter than its diff:
```python
import functools

import jax
import jax.numpy as jnp
from jax import lax
from jax.experimental import pallas as pl
from jax.experimental.pallas import tpu as pltpu
from jax.sharding import PartitionSpec as P

ITERS = 2
REACH = 4
NEAR = 2 * REACH
MESH = pl.DeviceIdType.MESH


def offset_of(i):
    return (i // 2 + 1) * (1 - 2 * (i % 2))


def mirror(i):
    return i + 1 - 2 * (i % 2)


def kernel(
    nv, no, amp_ref, drive_ref, blocks_ref, listed_ref, occ_ref, virt_ref, out_ref,
    blk, own, near, acc, inv, half, summed, rest, cur,
    blk_sem, loc_sem, a_send, a_recv, g_send, g_recv, p_send, p_recv, r_send, r_recv,
):
    v = lax.axis_index("vp")
    o = lax.axis_index("op")
    rows = amp_ref.shape[0]
    slots, width = blk.shape[0], blk.shape[1]
    pair = 2
    groups = no // pair
    side = o % pair
    group = o // pair
    partner = o + 1 - 2 * side

    for k in range(slots):
        pltpu.make_async_copy(blocks_ref.at[0, k], blk.at[k], blk_sem.at[k]).start()

    def exists(d):
        return jnp.logical_and(v + d >= 0, v + d < nv)

    barrier = pltpu.get_barrier_semaphore()
    count = jnp.int32(no - 1)
    for p in range(1, no):
        pl.semaphore_signal(barrier, inc=1, device_id=(v, (o + p) % no), device_id_type=MESH)
    for i in range(NEAR):
        d = offset_of(i)
        valid = exists(d)
        count = count + valid.astype(jnp.int32)

        @pl.when(valid)
        def _():
            pl.semaphore_signal(barrier, inc=1, device_id=(v + d, o), device_id_type=MESH)

    pl.semaphore_wait(barrier, count)

    def spread(it, src, p):
        to = (o + p) % no
        return pltpu.make_async_remote_copy(
            src_ref=src.at[:, pl.ds(pl.multiple_of(to * width, width), width)],
            dst_ref=own.at[it, pl.ds(pl.multiple_of(o * rows, rows), rows), :],
            send_sem=a_send.at[it, p],
            recv_sem=a_recv.at[it, p],
            device_id=(v, to),
            device_id_type=MESH,
        )

    def keep(it, src):
        return pltpu.make_async_copy(
            src.at[:, pl.ds(pl.multiple_of(o * width, width), width)],
            own.at[it, pl.ds(pl.multiple_of(o * rows, rows), rows), :],
            loc_sem.at[it],
        )

    def share(it, i):
        return pltpu.make_async_remote_copy(
            src_ref=own.at[it],
            dst_ref=near.at[it, mirror(i)],
            send_sem=g_send.at[it, i],
            recv_sem=g_recv.at[it, mirror(i)],
            device_id=(v + offset_of(i), o),
            device_id_type=MESH,
        )

    def arrived(it, i):
        return pltpu.make_async_remote_copy(
            src_ref=own.at[it],
            dst_ref=near.at[it, i],
            send_sem=g_send.at[it, i],
            recv_sem=g_recv.at[it, i],
            device_id=(v + offset_of(i), o),
            device_id_type=MESH,
        )

    def fold(it, j):
        return pltpu.make_async_remote_copy(
            src_ref=acc.at[it, pl.ds(pl.multiple_of((j * pair + 1 - side) * rows, rows), rows), :],
            dst_ref=half.at[it, j],
            send_sem=p_send.at[it, j],
            recv_sem=p_recv.at[it, j],
            device_id=(v, partner),
            device_id_type=MESH,
        )

    def settle(it, q):
        to = (group + q) % groups
        return pltpu.make_async_remote_copy(
            src_ref=summed.at[it, q],
            dst_ref=rest.at[it, q],
            send_sem=r_send.at[it, q],
            recv_sem=r_recv.at[it, q],
            device_id=(v, to * pair + side),
            device_id_type=MESH,
        )

    def weight(tile):
        slot = jnp.int32(0)
        hit = jnp.float32(0)
        for k in range(slots):
            same = listed_ref[0, k] == tile
            slot = jnp.where(same, k, slot)
            hit = jnp.where(same, jnp.float32(1), hit)
        return slot, hit

    def product(x, tile):
        slot, hit = weight(tile)
        x = x * jnp.full(x.shape, hit, jnp.float32).astype(x.dtype)
        return jnp.dot(x, blk[slot], preferred_element_type=jnp.float32)

    for it in range(ITERS):
        src = amp_ref if it == 0 else cur
        for p in range(1, no):
            spread(it, src, p).start()
        keep(it, src).start()
        if it == 0:
            eye = lax.broadcasted_iota(jnp.int32, (rows, rows), 0) == lax.broadcasted_iota(
                jnp.int32, (rows, rows), 1
            )
            occ = jnp.sum(
                jnp.where(eye, jnp.broadcast_to(occ_ref[...], (rows, rows)), 0.0),
                axis=1,
                keepdims=True,
            )
            inv[...] = 1.0 / (occ + virt_ref[...])
        keep(it, src).wait()
        for p in range(1, no):
            spread(it, src, p).wait_recv()
        for i in range(NEAR):

            @pl.when(exists(offset_of(i)))
            def _():
                share(it, i).start()

        if it == 0:
            for k in range(slots):
                pltpu.make_async_copy(blocks_ref.at[0, k], blk.at[k], blk_sem.at[k]).wait()
        acc[it] = product(own[it], v)

        def step(i, carry):
            @pl.when(exists(offset_of(i)))
            def _():
                arrived(it, i).wait_recv()
                acc[it] += product(near[it, i], v + offset_of(i))

            return carry

        lax.fori_loop(0, NEAR, step, 0)

        for q in range(1, groups + 1):
            fold(it, (group + q) % groups).start()
        for q in range(1, groups + 1):
            j = (group + q) % groups
            fold(it, j).wait_recv()
            total = acc[it, pl.ds(pl.multiple_of((j * pair + side) * rows, rows), rows), :] + half[it, j]
            if q < groups:
                summed[it, q] = total
                settle(it, q).start()
        for q in range(1, groups):
            settle(it, q).wait_recv()
            total = total + rest[it, q]
        value = ((drive_ref[...].astype(jnp.float32) + total) * inv[...]).astype(jnp.bfloat16)
        if it == ITERS - 1:
            out_ref[...] = value
        else:
            cur[...] = value

    for it in range(ITERS):
        src = amp_ref if it == 0 else cur
        for p in range(1, no):
            spread(it, src, p).wait_send()
        for i in range(NEAR):

            @pl.when(exists(offset_of(i)))
            def _():
                share(it, i).wait_send()

        for j in range(groups):
            fold(it, j).wait_send()
        for q in range(1, groups):
            settle(it, q).wait_send()


def per_device(nv, no, amplitudes, driving_term, blocks, block_tile, occupied_energy, virtual_energy):
    rows, cols = amplitudes.shape
    slots, width = blocks.shape[1], blocks.shape[2]
    groups = no // 2
    dma = pltpu.SemaphoreType.DMA
    vmem = pl.BlockSpec(memory_space=pltpu.VMEM)
    return pl.pallas_call(
        functools.partial(kernel, nv, no),
        out_shape=jax.ShapeDtypeStruct((rows, cols), jnp.bfloat16),
        in_specs=[
            vmem,
            vmem,
            pl.BlockSpec(memory_space=pl.ANY),
            pl.BlockSpec(memory_space=pltpu.SMEM),
            vmem,
            vmem,
        ],
        out_specs=vmem,
        scratch_shapes=[
            pltpu.VMEM((slots, width, cols), jnp.bfloat16),
            pltpu.VMEM((ITERS, no * rows, width), jnp.bfloat16),
            pltpu.VMEM((ITERS, NEAR, no * rows, width), jnp.bfloat16),
            pltpu.VMEM((ITERS, no * rows, cols), jnp.float32),
            pltpu.VMEM((rows, cols), jnp.float32),
            pltpu.VMEM((ITERS, groups, rows, cols), jnp.float32),
            pltpu.VMEM((ITERS, groups, rows, cols), jnp.float32),
            pltpu.VMEM((ITERS, groups, rows, cols), jnp.float32),
            pltpu.VMEM((rows, cols), jnp.bfloat16),
            dma((slots,)),
            dma((ITERS,)),
            dma((ITERS, no)),
            dma((ITERS, no)),
            dma((ITERS, NEAR)),
            dma((ITERS, NEAR)),
            dma((ITERS, groups)),
            dma((ITERS, groups)),
            dma((ITERS, groups)),
            dma((ITERS, groups)),
        ],
        compiler_params=pltpu.CompilerParams(
            collective_id=0, has_side_effects=True, vmem_limit_bytes=40 << 20
        ),
    )(
        amplitudes,
        driving_term,
        blocks,
        block_tile,
        occupied_energy.reshape(1, rows),
        virtual_energy.reshape(1, cols),
    )


def solution(mesh):
    in_specs = (
        P("op", "vp"),
        P("op", "vp"),
        P("vp", None, "op", None),
        P("vp", None),
        P("op"),
        P("vp"),
    )
    return jax.shard_map(
        functools.partial(per_device, mesh.shape["vp"], mesh.shape["op"]),
        mesh=mesh,
        in_specs=in_specs,
        out_specs=P("op", "vp"),
        check_vma=False,
    )
```

time: 148 us -> 48.6 us (0.33)
  blocking collectives: 78 us -> 0 us
  waiting for transfers between devices: 43.7 us -> 0 us
  Pallas kernels: 0 us -> 41.8 us
  between operations: 13.4 us -> 0.02 us
  matrix products: 8.92 us -> 0 us
  local copies, waits for them, and re-layouts: 0.9 us -> 6.49 us
  other arithmetic: 2.62 us -> 0 us
    all_gather x2 -> x0, blocking collectives: 63.4 us -> none  [gather_listed(): shards = lax.all_gather(slices[None], 'vp', axis=0, tiled=True)]
    reduce_scatter x2 -> x0, waiting for transfers between devices: 43.7 us -> none  [per_device(): lax.psum_scatter(partial_value, 'op', scatter_dimension=0, tiled=True)]
    pallas_call x0 -> x1, Pallas kernels: none -> 41.8 us  [per_device(): pl.pallas_call(functools.partial(kernel, nv, no), out_shape=jax.ShapeDtyp...]
    all_to_all x2 -> x0, blocking collectives: 14.7 us -> none  [per_device(): lax.all_to_all(current, 'op', split_axis=1, concat_axis=0, tiled=True)]
    dot_general x4 -> x0, matrix products: 8.92 us -> none  [the longest x2 7.43 us: per_device(): jnp.einsum('kmc,kcn->mn', chosen, integral_panel, preferred_element_type=...]
    unnamed x8 -> x13, local copies, waits for them, and re-layouts: 0.01 us -> 6.49 us
    convert_element_type x2 -> x0, other arithmetic: 2.62 us -> none  [per_device(): current = ((driving + ladder) * inverse).astype(jnp.bfloat16)]
  transfers between devices with their start and end apart: 2 -> 0, of which waited for: 2 -> 0; matrix products, arithmetic and copies ran while one was open for 0% -> 0% of each run, Pallas kernels for 0% -> 0%
where the time goes in v1:
time: 48.6 us; the launch traced here: 48.3 us
  Pallas kernels  41.8 us (86%)
  local copies, waits for them, and re-layouts  6.49 us (13%)
    pallas_call x1, Pallas kernels, per_device(): pl.pallas_call(functools.partial(kernel, nv, no), out_shape=jax.ShapeDtyp...  41.8 us
    unnamed x13, local copies, waits for them, and re-layouts  6.49 us

profile of v1, /device:TPU:0, one launch (start us, length us, event | category | flops | bytes accessed | tf_op | source)
XLA Modules:
  0.0 48.3 jit_solution(4779100197098471845)
XLA Ops:
  0.0 0.0 copy-start
  0.0 2.2 %copy-done = bf16[1,8,256,1024]{3,2,1,0:T(8,128)(2,1)S(1)} copy-done((bf16[1,8,256,1024]{3,2,1,0:T(8,128)(2,1)S(1)}, bf16[1,8,256,1024]{3,2,1,0:T(8,128)(2,1)}, u32[]{:S(2)}) %copy-start) | copy-done | bytes 4194328
  2.2 0.0 copy-start.1
  2.2 0.8 %copy-done.1 = bf16[32,1024]{1,0:T(8,128)(2,1)S(1)} copy-done((bf16[32,1024]{1,0:T(8,128)(2,1)S(1)}, bf16[32,1024]{1,0:T(8,128)(2,1)}, u32[]{:S(2)}) %copy-start.1) | copy-done | bytes 65560
  3.0 0.0 copy-start.2
  3.0 0.8 %copy-done.2 = bf16[32,1024]{1,0:T(8,128)(2,1)S(1)} copy-done((bf16[32,1024]{1,0:T(8,128)(2,1)S(1)}, bf16[32,1024]{1,0:T(8,128)(2,1)}, u32[]{:S(2)}) %copy-start.2) | copy-done | bytes 65560
  3.9 0.0 copy-start.3
  3.9 0.7 %copy-done.3 = f32[1024]{0:T(1024)S(1)} copy-done((f32[1024]{0:T(1024)S(1)}, f32[1024]{0:T(1024)}, u32[]{:S(2)}) %copy-start.3) | copy-done | bytes 4120
  4.6 0.0 copy-start.4
  4.6 0.7 %copy-done.4 = s32[1,8]{1,0:T(1,128)S(1)} copy-done((s32[1,8]{1,0:T(1,128)S(1)}, s32[1,8]{1,0:T(1,128)}, u32[]{:S(2)}) %copy-start.4) | copy-done | bytes 56
  5.2 0.0 copy-start.5
  5.2 0.7 %copy-done.5 = f32[32]{0:T(128)S(1)} copy-done((f32[32]{0:T(128)S(1)}, f32[32]{0:T(128)}, u32[]{:S(2)}) %copy-start.5) | copy-done | bytes 152
  5.9 41.8 %shard_map.64 = bf16[32,1024]{1,0:T(8,128)(2,1)S(1)} custom-call(bf16[32,1024]{1,0:T(8,128)(2,1)S(1)} %copy-done.1, bf16[32,1024]{1,0:T(8,128)(2,1)S(1)} %copy-done.2, bf16[1,8,256,1024]{3,2,1,0:T(8,128)(2,1)S(1)} %copy-done, s32[1,8]{1,0:T(1,128)S(1)} %copy-done.4, f32[1,32]{1,0:T(1,128)S(1)} %bitcast.3, f32[1,1024]{1,0:T(1,128)S(1)} %bitcast.2), custom_call_target="tpu_custom_call" | custom-call | tf_op jit(solution)/shard_map/pallas_call | solution.py:212
  47.6 0.6 %copy.8 = bf16[32,1024]{1,0:T(8,128)(2,1)} copy(bf16[32,1024]{1,0:T(8,128)(2,1)S(1)} %shard_map.64) | data formatting | bytes 131072
Async XLA Ops:
  0.0 2.2 %copy-start = (bf16[1,8,256,1024]{3,2,1,0:T(8,128)(2,1)S(1)}, bf16[1,8,256,1024]{3,2,1,0:T(8,128)(2,1)}, u32[]{:S(2)}) copy-start(bf16[1,8,256,1024]{3,2,1,0:T(8,128)(2,1)} %blocks_ref.1) | copy-start | bytes 12582916
  2.2 0.8 %copy-start.1 = (bf16[32,1024]{1,0:T(8,128)(2,1)S(1)}, bf16[32,1024]{1,0:T(8,128)(2,1)}, u32[]{:S(2)}) copy-start(bf16[32,1024]{1,0:T(8,128)(2,1)} %amp_ref.1) | copy-start | bytes 196612
  3.0 0.8 %copy-start.2 = (bf16[32,1024]{1,0:T(8,128)(2,1)S(1)}, bf16[32,1024]{1,0:T(8,128)(2,1)}, u32[]{:S(2)}) copy-start(bf16[32,1024]{1,0:T(8,128)(2,1)} %drive_ref.1) | copy-start | bytes 196612
  3.9 0.7 %copy-start.3 = (f32[1024]{0:T(1024)S(1)}, f32[1024]{0:T(1024)}, u32[]{:S(2)}) copy-start(f32[1024]{0:T(1024)} %param.11) | copy-start | bytes 12292
  4.6 0.7 %copy-start.4 = (s32[1,8]{1,0:T(1,128)S(1)}, s32[1,8]{1,0:T(1,128)}, u32[]{:S(2)}) copy-start(s32[1,8]{1,0:T(1,128)} %listed_ref.1) | copy-start | bytes 100
  5.2 0.7 %copy-start.5 = (f32[32]{0:T(128)S(1)}, f32[32]{0:T(128)}, u32[]{:S(2)}) copy-start(f32[32]{0:T(128)} %param.10) | copy-start | bytes 388

commit v2 on v1

v2 whole, which is shorter than its diff:
```python
import functools

import jax
import jax.numpy as jnp
from jax import lax
from jax.experimental import pallas as pl
from jax.experimental.pallas import tpu as pltpu
from jax.sharding import PartitionSpec as P

ITERS = 2
REACH = 4
NEAR = 2 * REACH
MESH = pl.DeviceIdType.MESH


def offset_of(i):
    return (i // 2 + 1) * (1 - 2 * (i % 2))


def mirror(i):
    return i + 1 - 2 * (i % 2)


def kernel(
    nv, no, amp_ref, drive_ref, blocks_ref, listed_ref, occ_ref, virt_ref, out_ref,
    blk, own, near, acc, drive_rows, drive_cols, occ, virt, inv_rows, inv_cols,
    half_cols, summed_cols, rest_cols, half_rows, summed_rows, rest_rows,
    blk_sem, in_sem, loc_sem, a_send, a_recv, g_send, g_recv, p_send, p_recv, r_send, r_recv,
):
    v = lax.axis_index("vp")
    o = lax.axis_index("op")
    rows = amp_ref.shape[0]
    slots, width = blk.shape[0], blk.shape[1]
    pair = 2
    groups = no // pair
    side = o % pair
    group = o // pair
    partner = o + 1 - 2 * side

    def load_block(k):
        return pltpu.make_async_copy(blocks_ref.at[0, k], blk.at[k], blk_sem.at[k])

    loads = (
        pltpu.make_async_copy(virt_ref, virt, in_sem.at[0]),
        pltpu.make_async_copy(drive_ref, drive_rows, in_sem.at[1]),
    )
    for load in loads:
        load.start()
    for k in range(slots):
        load_block(k).start()

    def exists(d):
        return jnp.logical_and(v + d >= 0, v + d < nv)

    barrier = pltpu.get_barrier_semaphore()
    count = jnp.int32(no - 1)
    for p in range(1, no):
        pl.semaphore_signal(barrier, inc=1, device_id=(v, (o + p) % no), device_id_type=MESH)
    for i in range(NEAR):
        d = offset_of(i)
        valid = exists(d)
        count = count + valid.astype(jnp.int32)

        @pl.when(valid)
        def _():
            pl.semaphore_signal(barrier, inc=1, device_id=(v + d, o), device_id_type=MESH)

    pl.semaphore_wait(barrier, count)

    def my_rows(ref):
        return ref.at[pl.ds(pl.multiple_of(o * rows, rows), rows), :]

    def columns(ref, owner):
        return ref.at[:, pl.ds(pl.multiple_of(owner * width, width), width)]

    def pieces(to):
        return (
            (columns(amp_ref, to), my_rows(own.at[0])),
            (columns(drive_ref, to), my_rows(drive_cols)),
            (occ_ref, occ.at[o]),
        )

    def spread(n, p):
        to = (o + p) % no
        piece = pieces(to)[n]
        return pltpu.make_async_remote_copy(
            src_ref=piece[0],
            dst_ref=piece[1],
            send_sem=a_send.at[n, p],
            recv_sem=a_recv.at[n, p],
            device_id=(v, to),
            device_id_type=MESH,
        )

    def keep(n):
        piece = pieces(o)[n]
        return pltpu.make_async_copy(piece[0], piece[1], loc_sem.at[n])

    def share(it, i):
        return pltpu.make_async_remote_copy(
            src_ref=own.at[it],
            dst_ref=near.at[it, mirror(i)],
            send_sem=g_send.at[it, i],
            recv_sem=g_recv.at[it, mirror(i)],
            device_id=(v + offset_of(i), o),
            device_id_type=MESH,
        )

    def arrived(it, i):
        return pltpu.make_async_remote_copy(
            src_ref=own.at[it],
            dst_ref=near.at[it, i],
            send_sem=g_send.at[it, i],
            recv_sem=g_recv.at[it, i],
            device_id=(v + offset_of(i), o),
            device_id_type=MESH,
        )

    half = (half_cols, half_rows)
    summed = (summed_cols, summed_rows)
    rest = (rest_cols, rest_rows)

    def part(it, owner):
        if it < ITERS - 1:
            return acc.at[it, :, pl.ds(pl.multiple_of(owner * width, width), width)]
        return acc.at[it, pl.ds(pl.multiple_of(owner * rows, rows), rows), :]

    def fold(it, j):
        return pltpu.make_async_remote_copy(
            src_ref=part(it, j * pair + 1 - side),
            dst_ref=half[it].at[j],
            send_sem=p_send.at[it, j],
            recv_sem=p_recv.at[it, j],
            device_id=(v, partner),
            device_id_type=MESH,
        )

    def settle(it, q):
        to = (group + q) % groups
        return pltpu.make_async_remote_copy(
            src_ref=summed[it].at[q],
            dst_ref=rest[it].at[q],
            send_sem=r_send.at[it, q],
            recv_sem=r_recv.at[it, q],
            device_id=(v, to * pair + side),
            device_id_type=MESH,
        )

    def weight(tile):
        slot = jnp.int32(0)
        hit = jnp.float32(0)
        for k in range(slots):
            same = listed_ref[0, k] == tile
            slot = jnp.where(same, k, slot)
            hit = jnp.where(same, jnp.float32(1), hit)
        return slot, hit

    def product(x, tile):
        slot, hit = weight(tile)
        x = x * jnp.full(x.shape, hit, jnp.float32).astype(x.dtype)
        return jnp.dot(x, blk[slot], preferred_element_type=jnp.float32)

    def inverse(i, columns_of):
        eye = lax.broadcasted_iota(jnp.int32, (rows, rows), 0) == lax.broadcasted_iota(
            jnp.int32, (rows, rows), 1
        )
        energy = jnp.sum(
            jnp.where(eye, jnp.broadcast_to(occ[i], (rows, rows)), 0.0), axis=1, keepdims=True
        )
        return 1.0 / (energy + columns_of)

    for n in range(3):
        for p in range(1, no):
            spread(n, p).start()
        keep(n).start()
    keep(0).wait()
    for p in range(1, no):
        spread(0, p).wait_recv()

    for it in range(ITERS):
        for i in range(NEAR):

            @pl.when(exists(offset_of(i)))
            def _():
                share(it, i).start()

        if it == 0:
            for load in loads:
                load.wait()
            for n in range(1, 3):
                keep(n).wait()
                for p in range(1, no):
                    spread(n, p).wait_recv()
            mine = virt[:, pl.ds(pl.multiple_of(o * width, width), width)]
            for i in range(no):
                inv_cols[i * rows : (i + 1) * rows, :] = inverse(i, mine)
            inv_rows[...] = inverse(o, virt[...])
            for k in range(slots):
                load_block(k).wait()
        acc[it] = product(own[it], v)

        def step(i, carry):
            @pl.when(exists(offset_of(i)))
            def _():
                arrived(it, i).wait_recv()
                acc[it] += product(near[it, i], v + offset_of(i))

            return carry

        lax.fori_loop(0, NEAR, step, 0)

        for q in range(1, groups + 1):
            fold(it, (group + q) % groups).start()
        for q in range(1, groups + 1):
            j = (group + q) % groups
            fold(it, j).wait_recv()
            total = part(it, j * pair + side)[...] + half[it][j]
            if q < groups:
                summed[it][q] = total
                settle(it, q).start()
        for q in range(1, groups):
            settle(it, q).wait_recv()
            total = total + rest[it][q]
        if it == ITERS - 1:
            value = (drive_rows[...].astype(jnp.float32) + total) * inv_rows[...]
            out_ref[...] = value.astype(jnp.bfloat16)
        else:
            value = (drive_cols[...].astype(jnp.float32) + total) * inv_cols[...]
            own[it + 1] = value.astype(jnp.bfloat16)

    for n in range(3):
        for p in range(1, no):
            spread(n, p).wait_send()
    for it in range(ITERS):
        for i in range(NEAR):

            @pl.when(exists(offset_of(i)))
            def _():
                share(it, i).wait_send()

        for j in range(groups):
            fold(it, j).wait_send()
        for q in range(1, groups):
            settle(it, q).wait_send()


def per_device(nv, no, amplitudes, driving_term, blocks, block_tile, occupied_energy, virtual_energy):
    rows, cols = amplitudes.shape
    slots, width = blocks.shape[1], blocks.shape[2]
    groups = no // 2
    dma = pltpu.SemaphoreType.DMA
    hbm = pl.BlockSpec(memory_space=pltpu.HBM)
    return pl.pallas_call(
        functools.partial(kernel, nv, no),
        out_shape=jax.ShapeDtypeStruct((rows, cols), jnp.bfloat16),
        in_specs=[hbm, hbm, hbm, pl.BlockSpec(memory_space=pltpu.SMEM), hbm, hbm],
        out_specs=pl.BlockSpec(memory_space=pltpu.VMEM),
        scratch_shapes=[
            pltpu.VMEM((slots, width, cols), jnp.bfloat16),
            pltpu.VMEM((ITERS, no * rows, width), jnp.bfloat16),
            pltpu.VMEM((ITERS, NEAR, no * rows, width), jnp.bfloat16),
            pltpu.VMEM((ITERS, no * rows, cols), jnp.float32),
            pltpu.VMEM((rows, cols), jnp.bfloat16),
            pltpu.VMEM((no * rows, width), jnp.bfloat16),
            pltpu.VMEM((no, 1, rows), jnp.float32),
            pltpu.VMEM((1, cols), jnp.float32),
            pltpu.VMEM((rows, cols), jnp.float32),
            pltpu.VMEM((no * rows, width), jnp.float32),
        ]
        + [pltpu.VMEM((groups, no * rows, width), jnp.float32)] * 3
        + [pltpu.VMEM((groups, rows, cols), jnp.float32)] * 3
        + [
            dma((slots,)),
            dma((2,)),
            dma((3,)),
            dma((3, no)),
            dma((3, no)),
            dma((ITERS, NEAR)),
            dma((ITERS, NEAR)),
            dma((ITERS, groups)),
            dma((ITERS, groups)),
            dma((ITERS, groups)),
            dma((ITERS, groups)),
        ],
        compiler_params=pltpu.CompilerParams(
            collective_id=0, has_side_effects=True, vmem_limit_bytes=60 << 20
        ),
    )(
        amplitudes,
        driving_term,
        blocks,
        block_tile,
        occupied_energy.reshape(1, rows),
        virtual_energy.reshape(1, cols),
    )


def solution(mesh):
    in_specs = (
        P("op", "vp"),
        P("op", "vp"),
        P("vp", None, "op", None),
        P("vp", None),
        P("op"),
        P("vp"),
    )
    return jax.shard_map(
        functools.partial(per_device, mesh.shape["vp"], mesh.shape["op"]),
        mesh=mesh,
        in_specs=in_specs,
        out_specs=P("op", "vp"),
        check_vma=False,
    )
```

time: 48.6 us -> 41.4 us (0.85)
  local copies, waits for them, and re-layouts: 6.49 us -> 1.47 us
  Pallas kernels: 41.8 us -> 39.1 us
    unnamed x13 -> x1, local copies, waits for them, and re-layouts: 6.49 us -> 1.47 us
    pallas_call x1, Pallas kernels: 41.8 us -> 39.1 us  [per_device(): pl.pallas_call(functools.partial(kernel, nv, no), out_shape=jax.ShapeDtyp...]
where the time goes in v2:
time: 41.4 us; the launch traced here: 40.6 us
  Pallas kernels  39.1 us (94%)
  local copies, waits for them, and re-layouts  1.47 us (4%)
    pallas_call x1, Pallas kernels, per_device(): pl.pallas_call(functools.partial(kernel, nv, no), out_shape=jax.ShapeDtyp...  39.1 us
    unnamed x1, local copies, waits for them, and re-layouts  1.47 us

profile of v2, /device:TPU:0, one launch (start us, length us, event | category | flops | bytes accessed | tf_op | source)
XLA Modules:
  0.0 40.6 jit_solution(15746137463087944371)
XLA Ops:
  0.0 39.1 %shard_map.64 = bf16[32,1024]{1,0:T(8,128)(2,1)} custom-call(bf16[32,1024]{1,0:T(8,128)(2,1)} %amp_ref.1, bf16[32,1024]{1,0:T(8,128)(2,1)} %drive_ref.1, bf16[1,8,256,1024]{3,2,1,0:T(8,128)(2,1)} %blocks_ref.1, s32[1,8]{1,0:T(1,128)} %listed_ref.1, f32[1,32]{1,0:T(1,128)} %bitcast.3, f32[1,1024]{1,0:T(1,128)} %bitcast.2), custom_call_target="tpu_custom_call" | custom-call | tf_op jit(solution)/shard_map/pallas_call | solution.py:253
  39.2 1.5 %copy.8 = bf16[32,1024]{1,0:T(8,128)(2,1)} copy(bf16[32,1024]{1,0:T(8,128)(2,1)} %shard_map.64) | data formatting | bytes 131072

commit v3 on v2

--- a/solution.py
+++ b/solution.py
@@ -10,22 +10,19 @@
 ITERS = 2
 REACH = 4
 NEAR = 2 * REACH
+CUT = 5
 MESH = pl.DeviceIdType.MESH
 
 
-def offset_of(i):
-    return (i // 2 + 1) * (1 - 2 * (i % 2))
-
-
-def mirror(i):
-    return i + 1 - 2 * (i % 2)
+def index_of(e):
+    return 2 * (abs(e) - 1) + jnp.int32(e < 0)
 
 
 def kernel(
     nv, no, amp_ref, drive_ref, blocks_ref, listed_ref, occ_ref, virt_ref, out_ref,
-    blk, own, near, acc, drive_rows, drive_cols, occ, virt, inv_rows, inv_cols,
+    blk, own, near, acc, drive_rows, drive_cols, amp, occ, virt, inv_rows, inv_cols,
     half_cols, summed_cols, rest_cols, half_rows, summed_rows, rest_rows,
-    blk_sem, in_sem, loc_sem, a_send, a_recv, g_send, g_recv, p_send, p_recv, r_send, r_recv,
+    blk_sem, in_sem, loc_sem, a_send, a_recv, g_send, g_recv, f_send, f_recv, h_send, h_recv, p_send, p_recv, r_send, r_recv,
 ):
     v = lax.axis_index("vp")
     o = lax.axis_index("op")
@@ -36,6 +33,11 @@
     side = o % pair
     group = o // pair
     partner = o + 1 - 2 * side
+    total_rows = no * rows
+    w = 1 - 2 * (v % 2)
+    direct = (w, 2, -2, 4 * w, -4 * w)
+    passed = (2, -2, 4 * w)
+    cut = total_rows * CUT // 8 // 16 * 16
 
     def load_block(k):
         return pltpu.make_async_copy(blocks_ref.at[0, k], blk.at[k], blk_sem.at[k])
@@ -44,6 +46,8 @@
         pltpu.make_async_copy(virt_ref, virt, in_sem.at[0]),
         pltpu.make_async_copy(drive_ref, drive_rows, in_sem.at[1]),
     )
+    stage = pltpu.make_async_copy(amp_ref, amp, in_sem.at[2])
+    stage.start()
     for load in loads:
         load.start()
     for k in range(slots):
@@ -56,14 +60,13 @@
     count = jnp.int32(no - 1)
     for p in range(1, no):
         pl.semaphore_signal(barrier, inc=1, device_id=(v, (o + p) % no), device_id_type=MESH)
-    for i in range(NEAR):
-        d = offset_of(i)
-        valid = exists(d)
+    for e in direct:
+        valid = exists(e)
         count = count + valid.astype(jnp.int32)
 
         @pl.when(valid)
         def _():
-            pl.semaphore_signal(barrier, inc=1, device_id=(v + d, o), device_id_type=MESH)
+            pl.semaphore_signal(barrier, inc=1, device_id=(v + e, o), device_id_type=MESH)
 
     pl.semaphore_wait(barrier, count)
 
@@ -75,7 +78,7 @@
 
     def pieces(to):
         return (
-            (columns(amp_ref, to), my_rows(own.at[0])),
+            (columns(amp, to), my_rows(own.at[0])),
             (columns(drive_ref, to), my_rows(drive_cols)),
             (occ_ref, occ.at[o]),
         )
@@ -96,23 +99,43 @@
         piece = pieces(o)[n]
         return pltpu.make_async_copy(piece[0], piece[1], loc_sem.at[n])
 
-    def share(it, i):
+    def give(it, e, slot):
         return pltpu.make_async_remote_copy(
             src_ref=own.at[it],
-            dst_ref=near.at[it, mirror(i)],
-            send_sem=g_send.at[it, i],
-            recv_sem=g_recv.at[it, mirror(i)],
-            device_id=(v + offset_of(i), o),
-            device_id_type=MESH,
-        )
-
-    def arrived(it, i):
-        return pltpu.make_async_remote_copy(
-            src_ref=own.at[it],
-            dst_ref=near.at[it, i],
-            send_sem=g_send.at[it, i],
-            recv_sem=g_recv.at[it, i],
-            device_id=(v + offset_of(i), o),
+            dst_ref=near.at[it, slot],
+            send_sem=g_send.at[it, index_of(e)],
+            recv_sem=g_recv.at[it, slot],
+            device_id=(v + e, o),
+            device_id_type=MESH,
+        )
+
+    def share(it, e):
+        return give(it, e, index_of(-e))
+
+    def arrived(it, e):
+        return give(it, e, index_of(e))
+
+    def span(n):
+        return pl.ds(0, total_rows if n == 2 else cut)
+
+    def across(it, n, slot):
+        return pltpu.make_async_remote_copy(
+            src_ref=near.at[it, index_of(passed[n]), span(n), :],
+            dst_ref=near.at[it, slot, span(n), :],
+            send_sem=f_send.at[it, n],
+            recv_sem=f_recv.at[it, n],
+            device_id=(v + w, o),
+            device_id_type=MESH,
+        )
+
+    def along(it, n, m, slot):
+        low = pl.ds(cut, total_rows - cut)
+        return pltpu.make_async_remote_copy(
+            src_ref=near.at[it, index_of(w), low, :],
+            dst_ref=near.at[it, slot, low, :],
+            send_sem=h_send.at[it, n],
+            recv_sem=h_recv.at[it, m],
+            device_id=(v + passed[n], o),
             device_id_type=MESH,
         )
 
@@ -169,6 +192,7 @@
         )
         return 1.0 / (energy + columns_of)
 
+    stage.wait()
     for n in range(3):
         for p in range(1, no):
             spread(n, p).start()
@@ -178,11 +202,11 @@
         spread(0, p).wait_recv()
 
     for it in range(ITERS):
-        for i in range(NEAR):
-
-            @pl.when(exists(offset_of(i)))
-            def _():
-                share(it, i).start()
+        for e in direct:
+
+            @pl.when(exists(e))
+            def _():
+                share(it, e).start()
 
         if it == 0:
             for load in loads:
@@ -199,16 +223,39 @@
                 load_block(k).wait()
         acc[it] = product(own[it], v)
 
-        def step(i, carry):
-            @pl.when(exists(offset_of(i)))
-            def _():
-                arrived(it, i).wait_recv()
-                acc[it] += product(near[it, i], v + offset_of(i))
-
-            return carry
-
-        lax.fori_loop(0, NEAR, step, 0)
-
+        def add(e):
+            acc[it] += product(near[it, index_of(e)], v + e)
+
+        arrived(it, w).wait_recv()
+        for n in range(2):
+
+            @pl.when(exists(passed[n]))
+            def _():
+                along(it, n, 1 - n, index_of(w - passed[n])).start()
+
+        add(w)
+        for n in range(3):
+
+            @pl.when(exists(passed[n]))
+            def _():
+                arrived(it, passed[n]).wait_recv()
+                across(it, n, index_of(passed[n] - w)).start()
+                add(passed[n])
+
+        @pl.when(exists(-4 * w))
+        def _():
+            arrived(it, -4 * w).wait_recv()
+            add(-4 * w)
+
+        for n in range(3):
+            far = -3 * w if n == 2 else passed[n] + w
+
+            @pl.when(exists(far))
+            def _():
+                across(it, n, index_of(far)).wait_recv()
+                if n < 2:
+                    along(it, n, n, index_of(far)).wait_recv()
+                add(far)
         for q in range(1, groups + 1):
             fold(it, (group + q) % groups).start()
         for q in range(1, groups + 1):
@@ -216,11 +263,11 @@
             fold(it, j).wait_recv()
             total = part(it, j * pair + side)[...] + half[it][j]
             if q < groups:
-                summed[it][q] = total
+                summed[it][q] = total.astype(jnp.bfloat16)
                 settle(it, q).start()
         for q in range(1, groups):
             settle(it, q).wait_recv()
-            total = total + rest[it][q]
+            total = total + rest[it][q].astype(jnp.float32)
         if it == ITERS - 1:
             value = (drive_rows[...].astype(jnp.float32) + total) * inv_rows[...]
             out_ref[...] = value.astype(jnp.bfloat16)
@@ -232,11 +279,19 @@
         for p in range(1, no):
             spread(n, p).wait_send()
     for it in range(ITERS):
-        for i in range(NEAR):
-
-            @pl.when(exists(offset_of(i)))
-            def _():
-                share(it, i).wait_send()
+        for e in direct:
+
+            @pl.when(exists(e))
+            def _():
+                share(it, e).wait_send()
+
+        for n in range(3):
+
+            @pl.when(exists(passed[n]))
+            def _():
+                across(it, n, index_of(passed[n] - w)).wait_send()
+                if n < 2:
+                    along(it, n, 1 - n, index_of(w - passed[n])).wait_send()
 
         for j in range(groups):
             fold(it, j).wait_send()
@@ -249,6 +304,7 @@
     slots, width = blocks.shape[1], blocks.shape[2]
     groups = no // 2
     dma = pltpu.SemaphoreType.DMA
+    settled = (jnp.float32, jnp.bfloat16, jnp.bfloat16)
     hbm = pl.BlockSpec(memory_space=pltpu.HBM)
     return pl.pallas_call(
         functools.partial(kernel, nv, no),
@@ -262,21 +318,26 @@
             pltpu.VMEM((ITERS, no * rows, cols), jnp.float32),
             pltpu.VMEM((rows, cols), jnp.bfloat16),
             pltpu.VMEM((no * rows, width), jnp.bfloat16),
+            pltpu.VMEM((rows, cols), jnp.bfloat16),
             pltpu.VMEM((no, 1, rows), jnp.float32),
             pltpu.VMEM((1, cols), jnp.float32),
             pltpu.VMEM((rows, cols), jnp.float32),
             pltpu.VMEM((no * rows, width), jnp.float32),
         ]
-        + [pltpu.VMEM((groups, no * rows, width), jnp.float32)] * 3
-        + [pltpu.VMEM((groups, rows, cols), jnp.float32)] * 3
+        + [pltpu.VMEM((groups, no * rows, width), t) for t in settled]
+        + [pltpu.VMEM((groups, rows, cols), t) for t in settled]
         + [
             dma((slots,)),
-            dma((2,)),
+            dma((3,)),
             dma((3,)),
             dma((3, no)),
             dma((3, no)),
             dma((ITERS, NEAR)),
             dma((ITERS, NEAR)),
+            dma((ITERS, 3)),
+            dma((ITERS, 3)),
+            dma((ITERS, 2)),
+            dma((ITERS, 2)),
             dma((ITERS, groups)),
             dma((ITERS, groups)),
             dma((ITERS, groups)),

time: 41.4 us -> 37.3 us (0.901)
  the two profiles are of different devices: /device:TPU:0 before, /device:TPU:11 now
where the time goes in v3:
time: 37.3 us; the launch traced here: 37.2 us
  Pallas kernels  35.7 us (96%)
  local copies, waits for them, and re-layouts  1.47 us (4%)
    pallas_call x1, Pallas kernels, per_device(): pl.pallas_call(functools.partial(kernel, nv, no), out_shape=jax.ShapeDtyp...  35.7 us
    unnamed x1, local copies, waits for them, and re-layouts  1.47 us

profile of v3, /device:TPU:11, one launch (start us, length us, event | category | flops | bytes accessed | tf_op | source)
XLA Modules:
  0.0 37.2 jit_solution(11214511287546486580)
XLA Ops:
  0.0 35.7 %shard_map.64 = bf16[32,1024]{1,0:T(8,128)(2,1)} custom-call(bf16[32,1024]{1,0:T(8,128)(2,1)} %amp_ref.1, bf16[32,1024]{1,0:T(8,128)(2,1)} %drive_ref.1, bf16[1,8,256,1024]{3,2,1,0:T(8,128)(2,1)} %blocks_ref.1, s32[1,8]{1,0:T(1,128)} %listed_ref.1, f32[1,32]{1,0:T(1,128)} %bitcast.3, f32[1,1024]{1,0:T(1,128)} %bitcast.2), custom_call_target="tpu_custom_call" | custom-call | tf_op jit(solution)/shard_map/pallas_call | solution.py:309
  35.7 1.5 %copy.8 = bf16[32,1024]{1,0:T(8,128)(2,1)} copy(bf16[32,1024]{1,0:T(8,128)(2,1)} %shard_map.64) | data formatting | bytes 131072
